TPU v7x, 32 devices: a whole 2x2x4 slice. The times are simulated.
32 devices in a mesh: dp: 4 (over z), node: 2 (over y), chip: 4 (over x, core).
Axes of the slice: x: 2, y: 2, z: 4, core: 2. Of those that a mesh axis runs over, the one named last changes fastest.
Arguments:
- se_gate: bfloat16 [4096, 2048], P(('dp', 'node', 'chip')), parts along dimension 0, may hold values from -6 to 6
- se_key: bfloat16 [4096, 2048], P(('dp', 'node', 'chip')), parts along dimension 0, may hold values from -6 to 6
- se_value: bfloat16 [4096, 2048], P(('dp', 'node', 'chip')), parts along dimension 0, may hold values from -6 to 6
- li_gate: bfloat16 [4096, 2048], P(('dp', 'node', 'chip')), parts along dimension 0, may hold values from -6 to 6
- li_key: bfloat16 [4096, 2048], P(('dp', 'node', 'chip')), parts along dimension 0, may hold values from -6 to 6
- li_value: bfloat16 [4096, 2048], P(('dp', 'node', 'chip')), parts along dimension 0, may hold values from -6 to 6
- se_feature: float32 [3, 3, 2048], replicated, may hold values from -3 to 3
- se_filter: float32 [7, 2048], replicated, may hold values from -2 to 2
- li_feature: float32 [3, 3, 2048], replicated, may hold values from -3 to 3
- li_residue: float32 [16, 2048], replicated, may hold values from -1.25 to 1.25
- li_rate: float32 [16, 2048], replicated, may hold values from 4.8828125e-05 to 0.08, as said below
- li_skip: float32 [2048], replicated, may hold values from -4 to 4
Outputs:
- se_out: bfloat16 [4096, 2048], P(('dp', 'node', 'chip')), parts along dimension 0
- li_out: bfloat16 [4096, 2048], P(('dp', 'node', 'chip')), parts along dimension 0
There are 4 independent parts, one for each index of `dp`. A program takes and returns all parts, laid end to end along the dimension named above; an argument that names none is the same for every part. Nothing has to cross between parts.
Inputs may be any that keep to these rules, and one draw needn't show every extreme that they name: `li_rate`: positive decay rates.
All inputs are finite; a program needn't handle non-finite values.
Results may differ from a plain program's by a relative error of at most 0.0055.
Values may be sent and summed in bfloat16 or wider, within the bound.
A program may use at most 128 MiB of HBM per device.

v0:
```python
import functools

import jax
import jax.numpy as jnp
from jax import lax
from jax.experimental import pallas as pl
from jax.experimental.pallas import tpu as pltpu
from jax.sharding import PartitionSpec as P

LANES = 128
SUB = 8
LINK = jnp.bfloat16
GROUP = ("node", "chip")


def mixer(n, chips, *refs):
    streams, kept = refs[:6], refs[6:12]
    results = refs[12:14]
    (
        held, halo, arrived, sent, ext, extended, u_li, starts, full, terms, near, partial, gates, carried, own, inner, shift,
        se_feature, se_filter, li_feature, residue, rate, skip, in_sem, fixed_sem, halo_send, halo_recv, pair_send, pair_recv, state_send, state_recv,
    ) = refs[14:]
    rows, width = held.shape[1], held.shape[2]
    blocks = width // LANES
    chunks = rows // SUB
    modes = rate.shape[0]
    lags = se_filter.shape[0]
    pair = 2 if n % 2 == 0 else 1
    dp = lax.axis_index("dp")
    me = lax.axis_index("node") * chips + lax.axis_index("chip")

    def device(index):
        return (dp, lax.div(index, chips), lax.rem(index, chips))

    order = (4, 5, 1, 2, 0, 3)
    loads = [pltpu.make_async_copy(streams[i], held.at[i], in_sem.at[i]) for i in range(6)]
    fixed = (se_feature, se_filter, li_feature, residue, rate, skip)
    fixed_loads = [pltpu.make_async_copy(kept[i], fixed[i], fixed_sem.at[i]) for i in range(6)]
    for i in (4, 2):
        fixed_loads[i].start()
    for i in order:
        loads[i].start()
    for i in (3, 5, 0, 1):
        fixed_loads[i].start()

    barrier = pltpu.get_barrier_semaphore()

    @pl.loop(0, n)
    def _(other):
        @pl.when(other != me)
        def _():
            pl.semaphore_signal(barrier, inc=1, device_id=device(other), device_id_type=pl.DeviceIdType.MESH)

    for i in range(6):
        ext[i, pl.ds(0, 2 * SUB)] = jnp.zeros((2 * SUB, LANES), jnp.float32)

    def columns(c):
        return pl.ds(pl.multiple_of(c * LANES, LANES), LANES)

    def featurized(i, c, taps, stream, early):
        cols = columns(c)
        if i not in (4, 5):
            ext[i, pl.ds(SUB, SUB)] = halo[i, :, cols].astype(jnp.float32)
        ext[i, pl.ds(2 * SUB, rows)] = held[i, :, cols].astype(jnp.float32)
        first, count = 2 * SUB - early, rows + early
        total = taps[0, pl.ds(stream, 1), cols] * ext[i, pl.ds(first, count)]
        for lag in (1, 2):
            total = total + taps[lag, pl.ds(stream, 1), cols] * ext[i, pl.ds(first - lag, count)]
        return total

    def local_states(c):
        cols = columns(c)
        product = featurized(4, c, li_feature, 1, 0) * featurized(5, c, li_feature, 2, 0)
        u_li[c, pl.ds(0, SUB)] = jnp.zeros((SUB, LANES), jnp.float32)
        u_li[c, pl.ds(SUB, rows)] = product.astype(jnp.bfloat16).astype(jnp.float32)
        pace = rate[:, cols]
        powers = [None] + [jnp.exp(-pace * float(k)) for k in range(1, SUB + 1)]
        state = jnp.zeros((modes, LANES), jnp.float32)
        for a in range(chunks):
            starts[c, a] = state
            new = jnp.broadcast_to(u_li[c, pl.ds(SUB + a * SUB + SUB - 1, 1)], (modes, LANES))
            for b in range(SUB - 1):
                new = new + powers[SUB - 1 - b] * u_li[c, pl.ds(SUB + a * SUB + b, 1)]
            state = powers[SUB] * state + new
        own[c] = state

    for i in (4, 2):
        fixed_loads[i].wait()
    loads[4].wait()
    loads[5].wait()
    ahead = blocks // 4

    @pl.loop(0, ahead)
    def _(c):
        local_states(c)

    pl.semaphore_wait(barrier, n - 1)

    def halo_copy(i):
        return pltpu.make_async_remote_copy(
            src_ref=streams[i].at[pl.ds(rows - SUB, SUB)],
            dst_ref=halo.at[i],
            send_sem=halo_send.at[i],
            recv_sem=halo_recv.at[i],
            device_id=device(lax.rem(me + 1, n)),
            device_id_type=pl.DeviceIdType.MESH,
        )

    @pl.when(me < n - 1)
    def _():
        for i in order:
            halo_copy(i).start()

    @pl.when(me == 0)
    def _():
        halo[...] = jnp.zeros_like(halo)

    if pair == 2:
        @pl.when(lax.rem(me, 2) == 0)
        def _():
            inner[...] = jnp.zeros_like(inner)


    place = lax.broadcasted_iota(jnp.int32, (SUB, LANES), 0)
    step = place.astype(jnp.float32)

    def ready(i):
        @pl.when(me > 0)
        def _():
            halo_copy(i).wait_recv()

    @pl.loop(ahead, blocks)
    def _(c):
        local_states(c)

    ready(4)
    ready(5)

    @pl.loop(0, blocks)
    def _(c):
        cols = columns(c)

        def opening(i, stream):
            ext[i, pl.ds(SUB, SUB)] = halo[i, :, cols].astype(jnp.float32)
            ext[i, pl.ds(2 * SUB, 2 * SUB)] = held[i, pl.ds(0, 2 * SUB), cols].astype(jnp.float32)
            total = li_feature[0, pl.ds(stream, 1), cols] * ext[i, pl.ds(2 * SUB, SUB)]
            for lag in (1, 2):
                total = total + li_feature[lag, pl.ds(stream, 1), cols] * ext[i, pl.ds(2 * SUB - lag, SUB)]
            return total

        right = (opening(4, 1) * opening(5, 2)).astype(jnp.bfloat16).astype(jnp.float32)
        extended[pl.ds(0, SUB)] = right - u_li[c, pl.ds(SUB, SUB)]
        u_li[c, pl.ds(SUB, SUB)] = right
        pace = rate[:, cols]
        moved = jnp.exp(-pace * float(SUB - 1)) * extended[pl.ds(0, 1)]
        moved = moved + jnp.exp(-pace * float(SUB - 2)) * extended[pl.ds(1, 1)]
        shift[c] = moved
        state = own[c] + jnp.exp(-pace * float(rows - SUB)) * moved
        own[c] = state
        sent[c] = state.astype(sent.dtype)

    def state_copy(source, target):
        return pltpu.make_async_remote_copy(
            src_ref=sent,
            dst_ref=arrived.at[source],
            send_sem=state_send.at[target],
            recv_sem=state_recv.at[source],
            device_id=device(target),
            device_id_type=pl.DeviceIdType.MESH,
        )

    def pair_copy():
        return pltpu.make_async_remote_copy(
            src_ref=sent,
            dst_ref=inner,
            send_sem=pair_send.at[0],
            recv_sem=pair_recv.at[0],
            device_id=device(me + 1 - 2 * lax.rem(me, 2)),
            device_id_type=pl.DeviceIdType.MESH,
        )

    if pair == 2:
        @pl.when(lax.rem(me, 2) == 0)
        def _():
            pair_copy().start()

    for i in (3, 5, 0, 1):
        fixed_loads[i].wait()

    @pl.loop(0, blocks)
    def _(c):
        cols = columns(c)
        pace = rate[:, cols]
        twice = 2.0 * pace
        small = twice * (1.0 - twice * (0.5 - twice * (1.0 / 6.0 - twice * (1.0 / 24.0 - twice * (1.0 / 120.0)))))
        gap = jnp.where(twice < 0.03125, small, 1.0 - jnp.exp(-twice))
        carried[c] = residue[:, cols] * jnp.sqrt(gap)
        total = jnp.zeros((SUB, LANES), jnp.float32)
        for m in range(modes):
            speed = rate[pl.ds(m, 1), cols]
            term = carried[c, pl.ds(m, 1)] * jnp.exp(-speed * step)
            total = total + term
            terms[c, m] = term * jnp.exp(-speed)
        near[c, 0] = total
        for lag in range(SUB - 1, -1, -1):
            tap = near[c, 0, pl.ds(lag, 1)]
            if lag == 0:
                tap = tap + skip[:, cols]
            near[c, lag] = jnp.where(place >= lag, jnp.broadcast_to(tap, (SUB, LANES)), 0.0)

    if pair == 2:
        @pl.when(lax.rem(me, 2) == 1)
        def _():
            pair_copy().wait_recv()

            @pl.loop(0, blocks)
            def _(c):
                fall = jnp.exp(-rate[:, columns(c)] * float(rows))
                sent[c] = (fall * inner[c].astype(jnp.float32) + own[c]).astype(sent.dtype)

    leads = lax.rem(me, pair) == pair - 1
    slot = lax.div(me, pair)

    @pl.when(leads)
    def _():
        @pl.loop(me + 1, n)
        def _(target):
            state_copy(slot, n + me - target).start()

    for i in (1, 2, 0, 3):
        loads[i].wait()
        ready(i)

    @pl.loop(0, blocks)
    def _(c):
        cols = columns(c)
        product = featurized(1, c, se_feature, 1, SUB) * featurized(2, c, se_feature, 2, SUB)
        extended[...] = product.astype(jnp.bfloat16).astype(jnp.float32)
        mixed = se_filter[pl.ds(0, 1), cols] * extended[pl.ds(SUB, rows)]
        for lag in range(1, lags):
            mixed = mixed + se_filter[pl.ds(lag, 1), cols] * extended[pl.ds(SUB - lag, rows)]
        results[0][:, cols] = (featurized(0, c, se_feature, 0, 0) * mixed).astype(jnp.bfloat16)
        gates[c] = featurized(3, c, li_feature, 0, 0)
        taps = [near[c, lag] for lag in range(SUB)]
        for a in range(chunks):
            total = taps[0] * u_li[c, pl.ds(SUB + a * SUB, SUB)]
            for lag in range(1, SUB):
                total = total + taps[lag] * u_li[c, pl.ds(SUB + a * SUB - lag, SUB)]
            partial[c, pl.ds(a * SUB, SUB)] = total

    odd = lax.rem(jnp.full((modes, LANES), me, jnp.int32), 2) == 1

    @pl.loop(0, slot)
    def _(source):
        state_copy(source, me).wait_recv()

    @pl.loop(0, blocks)
    def _(c):
        cols = columns(c)
        pace = rate[:, cols]
        fall = jnp.exp(-pace * float(rows * pair))

        def add(source, total):
            return fall * total + arrived[source, c].astype(jnp.float32)

        earlier = lax.fori_loop(0, slot, add, jnp.zeros((modes, LANES), jnp.float32))
        if pair == 2:
            within = jnp.exp(-pace * float(rows)) * earlier + inner[c].astype(jnp.float32)
            earlier = jnp.where(odd, within, earlier)
        hop = jnp.exp(-pace * float(SUB))
        for a in range(chunks):
            full[a] = starts[c, a] + earlier
            earlier = hop * earlier
            if a == 0:
                earlier = earlier + shift[c]
        for top in range(0, chunks, SUB):
            span = range(top, min(top + SUB, chunks))
            totals = [partial[c, pl.ds(a * SUB, SUB)] for a in span]
            for m in range(modes):
                term = terms[c, m]
                totals = [total + term * full[a, pl.ds(m, 1)] for a, total in zip(span, totals)]
            for a, total in zip(span, totals):
                partial[c, pl.ds(a * SUB, SUB)] = total
        results[1][:, cols] = (gates[c] * partial[c]).astype(jnp.bfloat16)

    @pl.when(me < n - 1)
    def _():
        for i in range(6):
            halo_copy(i).wait_send()

    if pair == 2:
        @pl.when(lax.rem(me, 2) == 0)
        def _():
            pair_copy().wait_send()

    @pl.when(leads)
    def _():
        @pl.loop(me + 1, n)
        def _(target):
            state_copy(slot, target).wait_send()


def publish(se, li, se_out, li_out, sems):
    copies = [
        pltpu.make_async_copy(se, se_out, sems.at[0]),
        pltpu.make_async_copy(li, li_out, sems.at[1]),
    ]
    for copy in copies:
        copy.start()
    for copy in copies:
        copy.wait()


def shards(*args):
    rows, width = args[0].shape
    modes = args[10].shape[0]
    n, chips = lax.axis_size(GROUP), lax.axis_size("chip")
    blocks, chunks = width // LANES, rows // SUB
    f32 = jnp.float32
    far = pl.BlockSpec(memory_space=pltpu.HBM)
    local = pl.BlockSpec(memory_space=pltpu.VMEM)
    operands = args[:11] + (args[11][None],)
    words = rows * width * 10 + width * modes * (3 * chunks + 3 * SUB + 8 + n)
    budget = min(4 * words + 8 * 2**20, 60 * 2**20)
    mixed = pl.pallas_call(
        functools.partial(mixer, n, chips),
        out_shape=(jax.ShapeDtypeStruct((rows, width), jnp.bfloat16),) * 2,
        in_specs=[far] * 12,
        out_specs=(local, local),
        scratch_shapes=[
            pltpu.VMEM((6, rows, width), jnp.bfloat16),
            pltpu.VMEM((6, SUB, width), jnp.bfloat16),
            pltpu.VMEM((n, blocks, modes, LANES), LINK),
            pltpu.VMEM((blocks, modes, LANES), LINK),
            pltpu.VMEM((6, rows + 2 * SUB, LANES), f32),
            pltpu.VMEM((rows + SUB, LANES), f32),
            pltpu.VMEM((blocks, rows + SUB, LANES), f32),
            pltpu.VMEM((blocks, chunks, modes, LANES), f32),
            pltpu.VMEM((chunks, modes, LANES), f32),
            pltpu.VMEM((blocks, modes, SUB, LANES), f32),
            pltpu.VMEM((blocks, SUB, SUB, LANES), f32),
            pltpu.VMEM((blocks, rows, LANES), f32),
            pltpu.VMEM((blocks, rows, LANES), f32),
            pltpu.VMEM((blocks, modes, LANES), f32),
            pltpu.VMEM((blocks, modes, LANES), f32),
            pltpu.VMEM((blocks, modes, LANES), LINK),
            pltpu.VMEM((blocks, modes, LANES), f32),
            *[pltpu.VMEM(array.shape, f32) for array in operands[6:]],
            pltpu.SemaphoreType.DMA((6,)),
            pltpu.SemaphoreType.DMA((6,)),
            pltpu.SemaphoreType.DMA((6,)),
            pltpu.SemaphoreType.DMA((6,)),
            pltpu.SemaphoreType.DMA((1,)),
            pltpu.SemaphoreType.DMA((1,)),
            pltpu.SemaphoreType.DMA((n,)),
            pltpu.SemaphoreType.DMA((n,)),
        ],
        compiler_params=pltpu.CompilerParams(collective_id=0, has_side_effects=True, vmem_limit_bytes=budget),
        name="mixer",
    )(*(pltpu.with_memory_space_constraint(array, pltpu.HBM) for array in operands))
    return pl.pallas_call(
        publish,
        out_shape=(jax.ShapeDtypeStruct((rows, width), jnp.bfloat16),) * 2,
        in_specs=[local, local],
        out_specs=(far, far),
        scratch_shapes=[pltpu.SemaphoreType.DMA((2,))],
        compiler_params=pltpu.CompilerParams(vmem_limit_bytes=8 * 2**20),
        name="publish",
    )(*mixed)


def solution(mesh):
    placed = (P(("dp", "node", "chip"), None),) * 6 + (P(),) * 6
    return jax.shard_map(
        shards,
        mesh=mesh,
        in_specs=placed,
        out_specs=(P(("dp", "node", "chip"), None), P(("dp", "node", "chip"), None)),
        check_vma=False,
    )
```

profile of v0, /device:TPU:4, one launch (start us, length us, event | category | flops | bytes accessed | tf_op | source)
XLA Modules:
  0.0 14.7 jit_solution(16292674935483560730)
XLA Ops:
  0.6 13.1 %mixer.1 = (bf16[128,2048]{1,0:T(8,128)(2,1)S(1)}, bf16[128,2048]{1,0:T(8,128)(2,1)S(1)}) custom-call(bf16[128,2048]{1,0:T(8,128)(2,1)} %refs_0_.1, bf16[128,2048]{1,0:T(8,128)(2,1)} %refs_1_.1, bf16[128,2048]{1,0:T(8,128)(2,1)} %refs_2_.1, bf16[128,2048]{1,0:T(8,128)(2,1)} %refs_3_.1, bf16[128,2048]{1,0:T(8,128)(2,1)} %refs_4_.1, ...), custom_call_target="tpu_custom_call" | custom-call | tf_op jit(solution)/shard_map/mixer/pallas_call | solution.py:325
  13.7 1.0 %publish.1 = (bf16[128,2048]{1,0:T(8,128)(2,1)}, bf16[128,2048]{1,0:T(8,128)(2,1)}) custom-call(bf16[128,2048]{1,0:T(8,128)(2,1)S(1)} %get-tuple-element.4.se, bf16[128,2048]{1,0:T(8,128)(2,1)S(1)} %get-tuple-element.5.li), custom_call_target="tpu_custom_call" | custom-call | tf_op jit(solution)/shard_map/publish/pallas_call | solution.py:361
where the time goes:
time: 14.9 us; the launch traced here: 14.7 us
  Pallas kernels  14.1 us (95%)
  between operations  0.64 us (4%)
    pallas_call x1, Pallas kernels, shards(): pl.pallas_call(functools.partial(mixer, n, chips), out_shape=(jax.ShapeDt...  13.1 us
    pallas_call x1, Pallas kernels, shards(): pl.pallas_call(publish, out_shape=(jax.ShapeDtypeStruct((rows, width), jn...  0.99 us

commit v1 on v0

--- a/solution.py
+++ b/solution.py
@@ -15,11 +15,11 @@
 
 def mixer(n, chips, *refs):
     streams, kept = refs[:6], refs[6:12]
-    results = refs[12:14]
+    se, partial, gates, terms, starts, shift, carry, hops = refs[12:20]
     (
-        held, halo, arrived, sent, ext, extended, u_li, starts, full, terms, near, partial, gates, carried, own, inner, shift,
-        se_feature, se_filter, li_feature, residue, rate, skip, in_sem, fixed_sem, halo_send, halo_recv, pair_send, pair_recv, state_send, state_recv,
-    ) = refs[14:]
+        held, halo, arrived, sent, ext, extended, u_li, near, carried, own, inner,
+        se_feature, se_filter, li_feature, residue, rate, skip, in_sem, part_sem, fixed_sem, halo_send, halo_recv, pair_send, pair_recv, state_send, state_recv,
+    ) = refs[20:]
     rows, width = held.shape[1], held.shape[2]
     blocks = width // LANES
     chunks = rows // SUB
@@ -33,15 +33,21 @@
         return (dp, lax.div(index, chips), lax.rem(index, chips))
 
     order = (4, 5, 1, 2, 0, 3)
-    loads = [pltpu.make_async_copy(streams[i], held.at[i], in_sem.at[i]) for i in range(6)]
+    parts = part_sem.shape[1]
+    each = width // parts
+    loads = [pltpu.make_async_copy(streams[i], held.at[i], in_sem.at[i]) for i in range(4)]
+
+    def piece(i, part):
+        cols = pl.ds(part * each, each)
+        return pltpu.make_async_copy(streams[i].at[:, cols], held.at[i, :, cols], part_sem.at[i - 4, part])
+
     fixed = (se_feature, se_filter, li_feature, residue, rate, skip)
     fixed_loads = [pltpu.make_async_copy(kept[i], fixed[i], fixed_sem.at[i]) for i in range(6)]
     for i in (4, 2):
         fixed_loads[i].start()
-    for i in order:
-        loads[i].start()
-    for i in (3, 5, 0, 1):
-        fixed_loads[i].start()
+    for part in range(parts):
+        for i in (4, 5):
+            piece(i, part).start()
 
     barrier = pltpu.get_barrier_semaphore()
 
@@ -84,16 +90,21 @@
             state = powers[SUB] * state + new
         own[c] = state
 
+    def stage(part):
+        for i in (4, 5):
+            piece(i, part).wait()
+
+        @pl.loop(part * (blocks // parts), (part + 1) * (blocks // parts))
+        def _(c):
+            local_states(c)
+
     for i in (4, 2):
         fixed_loads[i].wait()
-    loads[4].wait()
-    loads[5].wait()
-    ahead = blocks // 4
-
-    @pl.loop(0, ahead)
-    def _(c):
-        local_states(c)
-
+    for i in (3, 5, 0, 1):
+        fixed_loads[i].start()
+    stage(0)
+    for i in (1, 2, 0, 3):
+        loads[i].start()
     pl.semaphore_wait(barrier, n - 1)
 
     def halo_copy(i):
@@ -129,35 +140,41 @@
         def _():
             halo_copy(i).wait_recv()
 
-    @pl.loop(ahead, blocks)
-    def _(c):
-        local_states(c)
+    for part in range(1, parts):
+        stage(part)
 
     ready(4)
     ready(5)
 
-    @pl.loop(0, blocks)
-    def _(c):
+    wide = 4 if blocks % 4 == 0 else 1
+
+    def fixed_up(c, j):
         cols = columns(c)
 
         def opening(i, stream):
-            ext[i, pl.ds(SUB, SUB)] = halo[i, :, cols].astype(jnp.float32)
-            ext[i, pl.ds(2 * SUB, 2 * SUB)] = held[i, pl.ds(0, 2 * SUB), cols].astype(jnp.float32)
-            total = li_feature[0, pl.ds(stream, 1), cols] * ext[i, pl.ds(2 * SUB, SUB)]
+            at = 2 * j + i - 4
+            ext[at, pl.ds(SUB, SUB)] = halo[i, :, cols].astype(jnp.float32)
+            ext[at, pl.ds(2 * SUB, SUB)] = held[i, pl.ds(0, SUB), cols].astype(jnp.float32)
+            total = li_feature[0, pl.ds(stream, 1), cols] * ext[at, pl.ds(2 * SUB, SUB)]
             for lag in (1, 2):
-                total = total + li_feature[lag, pl.ds(stream, 1), cols] * ext[i, pl.ds(2 * SUB - lag, SUB)]
+                total = total + li_feature[lag, pl.ds(stream, 1), cols] * ext[at, pl.ds(2 * SUB - lag, SUB)]
             return total
 
         right = (opening(4, 1) * opening(5, 2)).astype(jnp.bfloat16).astype(jnp.float32)
-        extended[pl.ds(0, SUB)] = right - u_li[c, pl.ds(SUB, SUB)]
+        extended[pl.ds(j * SUB, SUB)] = right - u_li[c, pl.ds(SUB, SUB)]
         u_li[c, pl.ds(SUB, SUB)] = right
         pace = rate[:, cols]
-        moved = jnp.exp(-pace * float(SUB - 1)) * extended[pl.ds(0, 1)]
-        moved = moved + jnp.exp(-pace * float(SUB - 2)) * extended[pl.ds(1, 1)]
+        moved = jnp.exp(-pace * float(SUB - 1)) * extended[pl.ds(j * SUB, 1)]
+        moved = moved + jnp.exp(-pace * float(SUB - 2)) * extended[pl.ds(j * SUB + 1, 1)]
         shift[c] = moved
         state = own[c] + jnp.exp(-pace * float(rows - SUB)) * moved
         own[c] = state
         sent[c] = state.astype(sent.dtype)
+
+    @pl.loop(0, blocks // wide)
+    def _(many):
+        for j in range(wide):
+            fixed_up(many * wide + j, j)
 
     def state_copy(source, target):
         return pltpu.make_async_remote_copy(
@@ -239,7 +256,7 @@
         mixed = se_filter[pl.ds(0, 1), cols] * extended[pl.ds(SUB, rows)]
         for lag in range(1, lags):
             mixed = mixed + se_filter[pl.ds(lag, 1), cols] * extended[pl.ds(SUB - lag, rows)]
-        results[0][:, cols] = (featurized(0, c, se_feature, 0, 0) * mixed).astype(jnp.bfloat16)
+        se[:, cols] = (featurized(0, c, se_feature, 0, 0) * mixed).astype(jnp.bfloat16)
         gates[c] = featurized(3, c, li_feature, 0, 0)
         taps = [near[c, lag] for lag in range(SUB)]
         for a in range(chunks):
@@ -254,10 +271,8 @@
     def _(source):
         state_copy(source, me).wait_recv()
 
-    @pl.loop(0, blocks)
-    def _(c):
-        cols = columns(c)
-        pace = rate[:, cols]
+    def carried_in(c):
+        pace = rate[:, columns(c)]
         fall = jnp.exp(-pace * float(rows * pair))
 
         def add(source, total):
@@ -267,48 +282,69 @@
         if pair == 2:
             within = jnp.exp(-pace * float(rows)) * earlier + inner[c].astype(jnp.float32)
             earlier = jnp.where(odd, within, earlier)
-        hop = jnp.exp(-pace * float(SUB))
+        carry[c] = earlier
+        hops[c] = jnp.exp(-pace * float(SUB))
+
+    @pl.loop(0, blocks)
+    def _(c):
+        carried_in(c)
+
+    @pl.when(me < n - 1)
+    def _():
+        for i in range(6):
+            halo_copy(i).wait_send()
+
+    if pair == 2:
+        @pl.when(lax.rem(me, 2) == 0)
+        def _():
+            pair_copy().wait_send()
+
+    @pl.when(leads)
+    def _():
+        @pl.loop(me + 1, n)
+        def _(target):
+            state_copy(slot, target).wait_send()
+
+
+def finish(se, partial, gates, terms, starts, shift, carry, hops, se_out, li_out, made, full, sems):
+    blocks, rows = partial.shape[0], partial.shape[1]
+    chunks, modes = starts.shape[1], starts.shape[2]
+    parts = sems.shape[0] - 1
+    each = made.shape[1] // parts
+    whole = pltpu.make_async_copy(se, se_out, sems.at[parts])
+    whole.start()
+
+    def far(c):
+        earlier = carry[c]
+        hop = hops[c]
         for a in range(chunks):
             full[a] = starts[c, a] + earlier
             earlier = hop * earlier
             if a == 0:
                 earlier = earlier + shift[c]
+        cols = pl.ds(pl.multiple_of(c * LANES, LANES), LANES)
         for top in range(0, chunks, SUB):
             span = range(top, min(top + SUB, chunks))
             totals = [partial[c, pl.ds(a * SUB, SUB)] for a in span]
             for m in range(modes):
                 term = terms[c, m]
                 totals = [total + term * full[a, pl.ds(m, 1)] for a, total in zip(span, totals)]
-            for a, total in zip(span, totals):
-                partial[c, pl.ds(a * SUB, SUB)] = total
-        results[1][:, cols] = (gates[c] * partial[c]).astype(jnp.bfloat16)
-
-    @pl.when(me < n - 1)
-    def _():
-        for i in range(6):
-            halo_copy(i).wait_send()
-
-    if pair == 2:
-        @pl.when(lax.rem(me, 2) == 0)
-        def _():
-            pair_copy().wait_send()
-
-    @pl.when(leads)
-    def _():
-        @pl.loop(me + 1, n)
-        def _(target):
-            state_copy(slot, target).wait_send()
-
-
-def publish(se, li, se_out, li_out, sems):
-    copies = [
-        pltpu.make_async_copy(se, se_out, sems.at[0]),
-        pltpu.make_async_copy(li, li_out, sems.at[1]),
-    ]
-    for copy in copies:
-        copy.start()
-    for copy in copies:
-        copy.wait()
+            first = pl.ds(top * SUB, len(span) * SUB)
+            made[first, cols] = (gates[c, first] * jnp.concatenate(totals)).astype(jnp.bfloat16)
+
+    def piece(part):
+        cols = pl.ds(part * each, each)
+        return pltpu.make_async_copy(made.at[:, cols], li_out.at[:, cols], sems.at[part])
+
+    for part in range(parts):
+        @pl.loop(part * (blocks // parts), (part + 1) * (blocks // parts))
+        def _(c):
+            far(c)
+
+        piece(part).start()
+    for part in range(parts):
+        piece(part).wait()
+    whole.wait()
 
 
 def shards(*args):
@@ -322,31 +358,28 @@
     operands = args[:11] + (args[11][None],)
     words = rows * width * 10 + width * modes * (3 * chunks + 3 * SUB + 8 + n)
     budget = min(4 * words + 8 * 2**20, 60 * 2**20)
+    parts = 4 if blocks % 4 == 0 else 1
+    passed = ((rows, width), jnp.bfloat16), *(((blocks, *shape, LANES), f32) for shape in ((rows,), (rows,), (modes, SUB), (chunks, modes), (modes,), (modes,), (modes,)))
     mixed = pl.pallas_call(
         functools.partial(mixer, n, chips),
-        out_shape=(jax.ShapeDtypeStruct((rows, width), jnp.bfloat16),) * 2,
+        out_shape=tuple(jax.ShapeDtypeStruct(*one) for one in passed),
         in_specs=[far] * 12,
-        out_specs=(local, local),
+        out_specs=(local,) * len(passed),
         scratch_shapes=[
             pltpu.VMEM((6, rows, width), jnp.bfloat16),
             pltpu.VMEM((6, SUB, width), jnp.bfloat16),
             pltpu.VMEM((n, blocks, modes, LANES), LINK),
             pltpu.VMEM((blocks, modes, LANES), LINK),
-            pltpu.VMEM((6, rows + 2 * SUB, LANES), f32),
+            pltpu.VMEM((8, rows + 2 * SUB, LANES), f32),
             pltpu.VMEM((rows + SUB, LANES), f32),
             pltpu.VMEM((blocks, rows + SUB, LANES), f32),
-            pltpu.VMEM((blocks, chunks, modes, LANES), f32),
-            pltpu.VMEM((chunks, modes, LANES), f32),
-            pltpu.VMEM((blocks, modes, SUB, LANES), f32),
             pltpu.VMEM((blocks, SUB, SUB, LANES), f32),
-            pltpu.VMEM((blocks, rows, LANES), f32),
-            pltpu.VMEM((blocks, rows, LANES), f32),
             pltpu.VMEM((blocks, modes, LANES), f32),
             pltpu.VMEM((blocks, modes, LANES), f32),
             pltpu.VMEM((blocks, modes, LANES), LINK),
-            pltpu.VMEM((blocks, modes, LANES), f32),
             *[pltpu.VMEM(array.shape, f32) for array in operands[6:]],
-            pltpu.SemaphoreType.DMA((6,)),
+            pltpu.SemaphoreType.DMA((4,)),
+            pltpu.SemaphoreType.DMA((2, parts)),
             pltpu.SemaphoreType.DMA((6,)),
             pltpu.SemaphoreType.DMA((6,)),
             pltpu.SemaphoreType.DMA((6,)),
@@ -359,13 +392,17 @@
         name="mixer",
     )(*(pltpu.with_memory_space_constraint(array, pltpu.HBM) for array in operands))
     return pl.pallas_call(
-        publish,
+        finish,
         out_shape=(jax.ShapeDtypeStruct((rows, width), jnp.bfloat16),) * 2,
-        in_specs=[local, local],
+        in_specs=[local] * len(passed),
         out_specs=(far, far),
-        scratch_shapes=[pltpu.SemaphoreType.DMA((2,))],
+        scratch_shapes=[
+            pltpu.VMEM((rows, width), jnp.bfloat16),
+            pltpu.VMEM((chunks, modes, LANES), f32),
+            pltpu.SemaphoreType.DMA((parts + 1,)),
+        ],
         compiler_params=pltpu.CompilerParams(vmem_limit_bytes=8 * 2**20),
-        name="publish",
+        name="finish",
     )(*mixed)
 
 

time: 14.9 us -> 14.3 us (0.960)
  Pallas kernels: 14.1 us -> 13.5 us
    pallas_call x2, Pallas kernels: 14.1 us -> 13.5 us  [the longest x1 11.3 us: shards(): pl.pallas_call(functools.partial(mixer, n, chips), out_shape=tuple((jax.S...]
where the time goes in v1:
time: 14.3 us; the launch traced here: 14.1 us
  Pallas kernels  13.5 us (94%)
  between operations  0.64 us (4%)
    pallas_call x1, Pallas kernels, shards(): pl.pallas_call(functools.partial(mixer, n, chips), out_shape=tuple((jax.S...  11.3 us
    pallas_call x1, Pallas kernels, shards(): pl.pallas_call(finish, out_shape=(jax.ShapeDtypeStruct((rows, width), jnp...  2.21 us

profile of v1, /device:TPU:4, one launch (start us, length us, event | category | flops | bytes accessed | tf_op | source)
XLA Modules:
  0.0 14.1 jit_solution(12579228457764022575)
XLA Ops:
  0.6 11.3 %mixer.1 = (bf16[128,2048]{1,0:T(8,128)(2,1)S(1)}, f32[16,128,128]{2,1,0:T(8,128)S(1)}, f32[16,128,128]{2,1,0:T(8,128)S(1)}, f32[16,16,8,128]{3,2,1,0:T(8,128)S(...) custom-call(bf16[128,2048]{1,0:T(8,128)(2,1)} %refs_0_.1, ...), custom_call_target="tpu_custom_call" | custom-call | tf_op jit(solution)/shard_map/mixer/pallas_call | solution.py:363
  11.9 2.2 %finish.1 = (bf16[128,2048]{1,0:T(8,128)(2,1)}, bf16[128,2048]{1,0:T(8,128)(2,1)}) custom-call(bf16[128,2048]{1,0:T(8,128)(2,1)S(1)} %get-tuple-element.10.se, f32[16,128,128]{2,1,0:T(8,128)S(1)} %get-tuple-element.11.partial, f32[16,128,128]{2,1,0:T(8,128)S(1)} %get-tuple-element.12.gates, f32[16,16,8,128]{3,2,1,0:T(8,128)S(1)} %get-tuple-element.13.terms, ...), custom_call_target="tpu_custom_call" | custom-call | tf_op jit(solution)/shard_map/finish/pallas_call | solution.py:394

commit v2 on v1

--- a/solution.py
+++ b/solution.py
@@ -18,7 +18,7 @@
     se, partial, gates, terms, starts, shift, carry, hops = refs[12:20]
     (
         held, halo, arrived, sent, ext, extended, u_li, near, carried, own, inner,
-        se_feature, se_filter, li_feature, residue, rate, skip, in_sem, part_sem, fixed_sem, halo_send, halo_recv, pair_send, pair_recv, state_send, state_recv,
+        se_feature, se_filter, li_feature, residue, rate, skip, in_sem, part_sem, fixed_sem, halo_send, halo_recv, pair_send, pair_recv, state_send, state_recv, ready_sem,
     ) = refs[20:]
     rows, width = held.shape[1], held.shape[2]
     blocks = width // LANES
@@ -51,11 +51,32 @@
 
     barrier = pltpu.get_barrier_semaphore()
 
-    @pl.loop(0, n)
-    def _(other):
-        @pl.when(other != me)
-        def _():
-            pl.semaphore_signal(barrier, inc=1, device_id=device(other), device_id_type=pl.DeviceIdType.MESH)
+    odd_core = lax.rem(me, 2) == 1
+
+    def hail(semaphore, other):
+        pl.semaphore_signal(semaphore, inc=1, device_id=device(other), device_id_type=pl.DeviceIdType.MESH)
+
+    def hail_if(condition, semaphore, other):
+        @pl.when(condition)
+        def _():
+            hail(semaphore, other)
+
+    if pair == 2:
+        hail_if(me > 0, barrier, me - 1)
+        hail_if(odd_core & (me > 1), barrier, me - 2)
+        hail_if(odd_core & (me < n - 1), barrier, me + 2)
+    else:
+        @pl.loop(0, n)
+        def _(other):
+            hail_if(other != me, barrier, other)
+
+    def meet():
+        if pair == 2:
+            pl.semaphore_wait(barrier, jnp.where(odd_core, 2 * (me < n - 1).astype(jnp.int32) + (me > 1).astype(jnp.int32), 1))
+            if n > 4:
+                hail_if(me == n - 3, ready_sem, me - 2)
+        else:
+            pl.semaphore_wait(barrier, n - 1)
 
     for i in range(6):
         ext[i, pl.ds(0, 2 * SUB)] = jnp.zeros((2 * SUB, LANES), jnp.float32)
@@ -90,23 +111,6 @@
             state = powers[SUB] * state + new
         own[c] = state
 
-    def stage(part):
-        for i in (4, 5):
-            piece(i, part).wait()
-
-        @pl.loop(part * (blocks // parts), (part + 1) * (blocks // parts))
-        def _(c):
-            local_states(c)
-
-    for i in (4, 2):
-        fixed_loads[i].wait()
-    for i in (3, 5, 0, 1):
-        fixed_loads[i].start()
-    stage(0)
-    for i in (1, 2, 0, 3):
-        loads[i].start()
-    pl.semaphore_wait(barrier, n - 1)
-
     def halo_copy(i):
         return pltpu.make_async_remote_copy(
             src_ref=streams[i].at[pl.ds(rows - SUB, SUB)],
@@ -117,10 +121,40 @@
             device_id_type=pl.DeviceIdType.MESH,
         )
 
-    @pl.when(me < n - 1)
-    def _():
-        for i in order:
-            halo_copy(i).start()
+    per = blocks // parts
+
+    def states(first, last):
+        @pl.loop(first, last)
+        def _(c):
+            local_states(c)
+
+    for i in (4, 2):
+        fixed_loads[i].wait()
+    for part in range(parts):
+        for i in (4, 5):
+            piece(i, part).wait()
+        if part == 0:
+            for i in (3, 5, 0, 1):
+                fixed_loads[i].start()
+            for i in (1, 2, 0, 3):
+                loads[i].start()
+            states(0, per // 2)
+            meet()
+
+            @pl.when(me < n - 1)
+            def _():
+                for i in order:
+                    halo_copy(i).start()
+
+            states(per // 2, per)
+        else:
+            states(part * per, (part + 1) * per)
+
+    if pair == 2:
+        @pl.when(odd_core & (me > 1) & (me < n - 4))
+        def _():
+            pl.semaphore_wait(ready_sem, 1)
+            hail(ready_sem, me - 2)
 
     @pl.when(me == 0)
     def _():
@@ -139,9 +173,6 @@
         @pl.when(me > 0)
         def _():
             halo_copy(i).wait_recv()
-
-    for part in range(1, parts):
-        stage(part)
 
     ready(4)
     ready(5)
@@ -238,11 +269,24 @@
     leads = lax.rem(me, pair) == pair - 1
     slot = lax.div(me, pair)
 
-    @pl.when(leads)
-    def _():
-        @pl.loop(me + 1, n)
-        def _(target):
-            state_copy(slot, n + me - target).start()
+    def send_states(first, last):
+        @pl.when(leads)
+        def _():
+            @pl.loop(first, last)
+            def _(target):
+                state_copy(slot, target).start()
+
+    if pair == 2:
+        send_states(me + 1, jnp.minimum(me + 3, n))
+
+        if n > 4:
+            @pl.when(me == 1)
+            def _():
+                pl.semaphore_wait(ready_sem, 1)
+
+        send_states(me + 3, n)
+    else:
+        send_states(me + 1, n)
 
     for i in (1, 2, 0, 3):
         loads[i].wait()
@@ -387,6 +431,7 @@
             pltpu.SemaphoreType.DMA((1,)),
             pltpu.SemaphoreType.DMA((n,)),
             pltpu.SemaphoreType.DMA((n,)),
+            pltpu.SemaphoreType.REGULAR,
         ],
         compiler_params=pltpu.CompilerParams(collective_id=0, has_side_effects=True, vmem_limit_bytes=budget),
         name="mixer",

time: 14.3 us -> 13.9 us (0.972)
  the two profiles are of different devices: /device:TPU:4 before, /device:TPU:7 now
where the time goes in v2:
time: 13.9 us; the launch traced here: 13.7 us
  Pallas kernels  13.1 us (94%)
  between operations  0.64 us (5%)
    pallas_call x1, Pallas kernels, shards(): pl.pallas_call(functools.partial(mixer, n, chips), out_shape=tuple((jax.S...  10.9 us
    pallas_call x1, Pallas kernels, shards(): pl.pallas_call(finish, out_shape=(jax.ShapeDtypeStruct((rows, width), jnp...  2.21 us

profile of v2, /device:TPU:7, one launch (start us, length us, event | category | flops | bytes accessed | tf_op | source)
XLA Modules:
  0.0 13.7 jit_solution(4848115621413845871)
XLA Ops:
  0.6 10.9 %mixer.1 = (bf16[128,2048]{1,0:T(8,128)(2,1)S(1)}, f32[16,128,128]{2,1,0:T(8,128)S(1)}, f32[16,128,128]{2,1,0:T(8,128)S(1)}, f32[16,16,8,128]{3,2,1,0:T(8,128)S(...) custom-call(bf16[128,2048]{1,0:T(8,128)(2,1)} %refs_0_.1, ...), custom_call_target="tpu_custom_call" | custom-call | tf_op jit(solution)/shard_map/mixer/pallas_call | solution.py:407
  11.5 2.2 %finish.1 = (bf16[128,2048]{1,0:T(8,128)(2,1)}, bf16[128,2048]{1,0:T(8,128)(2,1)}) custom-call(bf16[128,2048]{1,0:T(8,128)(2,1)S(1)} %get-tuple-element.10.se, f32[16,128,128]{2,1,0:T(8,128)S(1)} %get-tuple-element.11.partial, f32[16,128,128]{2,1,0:T(8,128)S(1)} %get-tuple-element.12.gates, f32[16,16,8,128]{3,2,1,0:T(8,128)S(1)} %get-tuple-element.13.terms, ...), custom_call_target="tpu_custom_call" | custom-call | tf_op jit(solution)/shard_map/finish/pallas_call | solution.py:439

commit v3 on v2

--- a/solution.py
+++ b/solution.py
@@ -13,19 +13,44 @@
 GROUP = ("node", "chip")
 
 
+def paired(n, blocks):
+    return n % 2 == 0 and blocks % 2 == 0
+
+
+def far(c, partial, gates, terms, starts, shift, carry, hops, made, full):
+    chunks, modes = starts.shape[1], starts.shape[2]
+    earlier = carry[c]
+    hop = hops[c]
+    for a in range(chunks):
+        full[a] = starts[c, a] + earlier
+        earlier = hop * earlier
+        if a == 0:
+            earlier = earlier + shift[c]
+    cols = pl.ds(pl.multiple_of(c * LANES, LANES), LANES)
+    for top in range(0, chunks, SUB):
+        span = range(top, min(top + SUB, chunks))
+        totals = [partial[c, pl.ds(a * SUB, SUB)] for a in span]
+        for m in range(modes):
+            term = terms[c, m]
+            totals = [total + term * full[a, pl.ds(m, 1)] for a, total in zip(span, totals)]
+        first = pl.ds(top * SUB, len(span) * SUB)
+        made[first, cols] = (gates[c, first] * jnp.concatenate(totals)).astype(jnp.bfloat16)
+
+
 def mixer(n, chips, *refs):
     streams, kept = refs[:6], refs[6:12]
-    se, partial, gates, terms, starts, shift, carry, hops = refs[12:20]
+    se, made, partial, gates, terms, starts, shift, carry, hops = refs[12:21]
     (
-        held, halo, arrived, sent, ext, extended, u_li, near, carried, own, inner,
-        se_feature, se_filter, li_feature, residue, rate, skip, in_sem, part_sem, fixed_sem, halo_send, halo_recv, pair_send, pair_recv, state_send, state_recv, ready_sem,
-    ) = refs[20:]
+        held, halo, arrived, sent, ext, extended, u_li, near, carried, own, inner, tally, lent, full,
+        se_feature, se_filter, li_feature, residue, rate, skip, in_sem, part_sem, fixed_sem, halo_send, halo_recv, pair_send, pair_recv, state_send, state_recv, swap_send, swap_recv, ready_sem,
+    ) = refs[21:]
     rows, width = held.shape[1], held.shape[2]
     blocks = width // LANES
     chunks = rows // SUB
     modes = rate.shape[0]
     lags = se_filter.shape[0]
-    pair = 2 if n % 2 == 0 else 1
+    pair = 2 if paired(n, blocks) else 1
+    half = blocks // pair
     dp = lax.axis_index("dp")
     me = lax.axis_index("node") * chips + lax.axis_index("chip")
 
@@ -51,6 +76,7 @@
 
     barrier = pltpu.get_barrier_semaphore()
 
+    side = lax.rem(me, pair)
     odd_core = lax.rem(me, 2) == 1
 
     def hail(semaphore, other):
@@ -63,6 +89,7 @@
 
     if pair == 2:
         hail_if(me > 0, barrier, me - 1)
+        hail_if(jnp.logical_not(odd_core), barrier, me + 1)
         hail_if(odd_core & (me > 1), barrier, me - 2)
         hail_if(odd_core & (me < n - 1), barrier, me + 2)
     else:
@@ -72,7 +99,7 @@
 
     def meet():
         if pair == 2:
-            pl.semaphore_wait(barrier, jnp.where(odd_core, 2 * (me < n - 1).astype(jnp.int32) + (me > 1).astype(jnp.int32), 1))
+            pl.semaphore_wait(barrier, jnp.where(odd_core, 1 + 2 * (me < n - 1).astype(jnp.int32) + (me > 1).astype(jnp.int32), 1))
             if n > 4:
                 hail_if(me == n - 3, ready_sem, me - 2)
         else:
@@ -111,10 +138,12 @@
             state = powers[SUB] * state + new
         own[c] = state
 
+    tail = (2, SUB, SUB, 2, 2, 2)
+
     def halo_copy(i):
         return pltpu.make_async_remote_copy(
-            src_ref=streams[i].at[pl.ds(rows - SUB, SUB)],
-            dst_ref=halo.at[i],
+            src_ref=streams[i].at[pl.ds(rows - tail[i], tail[i])],
+            dst_ref=halo.at[i, pl.ds(SUB - tail[i], tail[i])],
             send_sem=halo_send.at[i],
             recv_sem=halo_recv.at[i],
             device_id=device(lax.rem(me + 1, n)),
@@ -209,8 +238,8 @@
 
     def state_copy(source, target):
         return pltpu.make_async_remote_copy(
-            src_ref=sent,
-            dst_ref=arrived.at[source],
+            src_ref=sent.at[pl.ds(lax.rem(target, pair) * half, half)],
+            dst_ref=arrived.at[source, pl.ds(lax.rem(target, pair) * half, half)],
             send_sem=state_send.at[target],
             recv_sem=state_recv.at[source],
             device_id=device(target),
@@ -243,6 +272,7 @@
         small = twice * (1.0 - twice * (0.5 - twice * (1.0 / 6.0 - twice * (1.0 / 24.0 - twice * (1.0 / 120.0)))))
         gap = jnp.where(twice < 0.03125, small, 1.0 - jnp.exp(-twice))
         carried[c] = residue[:, cols] * jnp.sqrt(gap)
+        hops[c] = jnp.exp(-pace * float(SUB))
         total = jnp.zeros((SUB, LANES), jnp.float32)
         for m in range(modes):
             speed = rate[pl.ds(m, 1), cols]
@@ -310,28 +340,77 @@
             partial[c, pl.ds(a * SUB, SUB)] = total
 
     odd = lax.rem(jnp.full((modes, LANES), me, jnp.int32), 2) == 1
+    step_by = 4 if half % 4 == 0 else 1
+
+    def by_four(first, body):
+        @pl.loop(0, half // step_by)
+        def _(many):
+            for j in range(step_by):
+                body(first + many * step_by + j)
+
+    def cleared(c):
+        tally[c] = jnp.zeros((modes, LANES), jnp.float32)
+
+    def summed(source):
+        def body(c):
+            fall = jnp.exp(-rate[:, columns(c)] * float(rows * pair))
+            tally[c] = fall * tally[c] + arrived[source, c].astype(jnp.float32)
+
+        return body
+
+    def lend(c):
+        lent[c] = tally[c].astype(lent.dtype)
+
+    def carried_in(c, before):
+        if pair == 2:
+            within = jnp.exp(-rate[:, columns(c)] * float(rows)) * before + inner[c].astype(jnp.float32)
+            before = jnp.where(odd, within, before)
+        carry[c] = before
+
+    ours, theirs = side * half, (pair - 1 - side) * half
+    by_four(ours, cleared)
 
     @pl.loop(0, slot)
     def _(source):
         state_copy(source, me).wait_recv()
-
-    def carried_in(c):
-        pace = rate[:, columns(c)]
-        fall = jnp.exp(-pace * float(rows * pair))
-
-        def add(source, total):
-            return fall * total + arrived[source, c].astype(jnp.float32)
-
-        earlier = lax.fori_loop(0, slot, add, jnp.zeros((modes, LANES), jnp.float32))
-        if pair == 2:
-            within = jnp.exp(-pace * float(rows)) * earlier + inner[c].astype(jnp.float32)
-            earlier = jnp.where(odd, within, earlier)
-        carry[c] = earlier
-        hops[c] = jnp.exp(-pace * float(SUB))
-
-    @pl.loop(0, blocks)
+        by_four(ours, summed(source))
+
+    def swap_copy(first):
+        return pltpu.make_async_remote_copy(
+            src_ref=lent.at[pl.ds(first, half)],
+            dst_ref=lent.at[pl.ds(first, half)],
+            send_sem=swap_send.at[0],
+            recv_sem=swap_recv.at[0],
+            device_id=device(me + 1 - 2 * lax.rem(me, 2)),
+            device_id_type=pl.DeviceIdType.MESH,
+        )
+
+    if pair == 2:
+        @pl.when(slot > 0)
+        def _():
+            by_four(ours, lend)
+            swap_copy(ours).start()
+
+        @pl.when(slot == 0)
+        def _():
+            lent[...] = jnp.zeros_like(lent)
+
+    by_four(ours, lambda c: carried_in(c, tally[c]))
+
+    @pl.loop(0, half)
     def _(c):
-        carried_in(c)
+        far(ours + c, partial, gates, terms, starts, shift, carry, hops, made, full)
+
+    if pair == 2:
+        @pl.when(slot > 0)
+        def _():
+            swap_copy(theirs).wait_recv()
+
+        by_four(theirs, lambda c: carried_in(c, lent[c].astype(jnp.float32)))
+
+        @pl.when(slot > 0)
+        def _():
+            swap_copy(ours).wait_send()
 
     @pl.when(me < n - 1)
     def _():
@@ -350,45 +429,35 @@
             state_copy(slot, target).wait_send()
 
 
-def finish(se, partial, gates, terms, starts, shift, carry, hops, se_out, li_out, made, full, sems):
-    blocks, rows = partial.shape[0], partial.shape[1]
-    chunks, modes = starts.shape[1], starts.shape[2]
-    parts = sems.shape[0] - 1
-    each = made.shape[1] // parts
-    whole = pltpu.make_async_copy(se, se_out, sems.at[parts])
-    whole.start()
-
-    def far(c):
-        earlier = carry[c]
-        hop = hops[c]
-        for a in range(chunks):
-            full[a] = starts[c, a] + earlier
-            earlier = hop * earlier
-            if a == 0:
-                earlier = earlier + shift[c]
-        cols = pl.ds(pl.multiple_of(c * LANES, LANES), LANES)
-        for top in range(0, chunks, SUB):
-            span = range(top, min(top + SUB, chunks))
-            totals = [partial[c, pl.ds(a * SUB, SUB)] for a in span]
-            for m in range(modes):
-                term = terms[c, m]
-                totals = [total + term * full[a, pl.ds(m, 1)] for a, total in zip(span, totals)]
-            first = pl.ds(top * SUB, len(span) * SUB)
-            made[first, cols] = (gates[c, first] * jnp.concatenate(totals)).astype(jnp.bfloat16)
-
-    def piece(part):
-        cols = pl.ds(part * each, each)
-        return pltpu.make_async_copy(made.at[:, cols], li_out.at[:, cols], sems.at[part])
-
-    for part in range(parts):
-        @pl.loop(part * (blocks // parts), (part + 1) * (blocks // parts))
-        def _(c):
-            far(c)
-
-        piece(part).start()
-    for part in range(parts):
-        piece(part).wait()
-    whole.wait()
+def finish(n, chips, se, made, partial, gates, terms, starts, shift, carry, hops, se_out, li_out, rest, full, sems):
+    blocks = partial.shape[0]
+    width = se.shape[1]
+    pair = 2 if paired(n, blocks) else 1
+    half = blocks // pair
+    me = lax.axis_index("node") * chips + lax.axis_index("chip")
+    ours = lax.rem(me, pair) * half
+    theirs = half - ours
+
+    def columns(first, count):
+        return pl.ds(pl.multiple_of(first * LANES, LANES), count * LANES)
+
+    own = columns(ours, half)
+    done = [pltpu.make_async_copy(se, se_out, sems.at[0]), pltpu.make_async_copy(made.at[:, own], li_out.at[:, own], sems.at[1])]
+    for copy in done:
+        copy.start()
+    if pair == 2:
+        parts = sems.shape[0] - 2
+        each = half // parts
+        for part in range(parts):
+            @pl.loop(part * each, (part + 1) * each)
+            def _(c):
+                far(theirs + c, partial, gates, terms, starts, shift, carry, hops, rest, full)
+
+            cols = columns(theirs + part * each, each)
+            done.append(pltpu.make_async_copy(rest.at[:, cols], li_out.at[:, cols], sems.at[2 + part]))
+            done[-1].start()
+    for copy in done:
+        copy.wait()
 
 
 def shards(*args):
@@ -403,7 +472,7 @@
     words = rows * width * 10 + width * modes * (3 * chunks + 3 * SUB + 8 + n)
     budget = min(4 * words + 8 * 2**20, 60 * 2**20)
     parts = 4 if blocks % 4 == 0 else 1
-    passed = ((rows, width), jnp.bfloat16), *(((blocks, *shape, LANES), f32) for shape in ((rows,), (rows,), (modes, SUB), (chunks, modes), (modes,), (modes,), (modes,)))
+    passed = ((rows, width), jnp.bfloat16), ((rows, width), jnp.bfloat16), *(((blocks, *shape, LANES), f32) for shape in ((rows,), (rows,), (modes, SUB), (chunks, modes), (modes,), (modes,), (modes,)))
     mixed = pl.pallas_call(
         functools.partial(mixer, n, chips),
         out_shape=tuple(jax.ShapeDtypeStruct(*one) for one in passed),
@@ -421,6 +490,9 @@
             pltpu.VMEM((blocks, modes, LANES), f32),
             pltpu.VMEM((blocks, modes, LANES), f32),
             pltpu.VMEM((blocks, modes, LANES), LINK),
+            pltpu.VMEM((blocks, modes, LANES), f32),
+            pltpu.VMEM((blocks, modes, LANES), LINK),
+            pltpu.VMEM((chunks, modes, LANES), f32),
             *[pltpu.VMEM(array.shape, f32) for array in operands[6:]],
             pltpu.SemaphoreType.DMA((4,)),
             pltpu.SemaphoreType.DMA((2, parts)),
@@ -431,20 +503,22 @@
             pltpu.SemaphoreType.DMA((1,)),
             pltpu.SemaphoreType.DMA((n,)),
             pltpu.SemaphoreType.DMA((n,)),
+            pltpu.SemaphoreType.DMA((1,)),
+            pltpu.SemaphoreType.DMA((1,)),
             pltpu.SemaphoreType.REGULAR,
         ],
         compiler_params=pltpu.CompilerParams(collective_id=0, has_side_effects=True, vmem_limit_bytes=budget),
         name="mixer",
     )(*(pltpu.with_memory_space_constraint(array, pltpu.HBM) for array in operands))
     return pl.pallas_call(
-        finish,
+        functools.partial(finish, n, chips),
         out_shape=(jax.ShapeDtypeStruct((rows, width), jnp.bfloat16),) * 2,
         in_specs=[local] * len(passed),
         out_specs=(far, far),
         scratch_shapes=[
             pltpu.VMEM((rows, width), jnp.bfloat16),
             pltpu.VMEM((chunks, modes, LANES), f32),
-            pltpu.SemaphoreType.DMA((parts + 1,)),
+            pltpu.SemaphoreType.DMA((2 + (2 if blocks % 4 == 0 else 1),)),
         ],
         compiler_params=pltpu.CompilerParams(vmem_limit_bytes=8 * 2**20),
         name="finish",

time: 13.9 us -> 12.6 us (0.906)
  the two profiles are of different devices: /device:TPU:7 before, /device:TPU:5 now
where the time goes in v3:
time: 12.6 us; the launch traced here: 12.4 us
  Pallas kernels  11.8 us (94%)
  between operations  0.64 us (5%)
    pallas_call x1, Pallas kernels, shards(): pl.pallas_call(functools.partial(mixer, n, chips), out_shape=tuple((jax.S...  10.3 us
    pallas_call x1, Pallas kernels, shards(): pl.pallas_call(functools.partial(finish, n, chips), out_shape=(jax.ShapeD...  1.46 us

profile of v3, /device:TPU:5, one launch (start us, length us, event | category | flops | bytes accessed | tf_op | source)
XLA Modules:
  0.0 12.4 jit_solution(1183236203776371613)
XLA Ops:
  0.6 10.3 %mixer.1 = (bf16[128,2048]{1,0:T(8,128)(2,1)S(1)}, bf16[128,2048]{1,0:T(8,128)(2,1)S(1)}, f32[16,128,128]{2,1,0:T(8,128)S(1)}, f32[16,128,128]{2,1,0:T(8,128)S(1...) custom-call(bf16[128,2048]{1,0:T(8,128)(2,1)} %refs_0_.1, ...), custom_call_target="tpu_custom_call" | custom-call | tf_op jit(solution)/shard_map/mixer/pallas_call | solution.py:476
  11.0 1.5 %finish.1 = (bf16[128,2048]{1,0:T(8,128)(2,1)}, bf16[128,2048]{1,0:T(8,128)(2,1)}) custom-call(bf16[128,2048]{1,0:T(8,128)(2,1)S(1)} %get-tuple-element.11.se, bf16[128,2048]{1,0:T(8,128)(2,1)S(1)} %get-tuple-element.12.made, f32[16,128,128]{2,1,0:T(8,128)S(1)} %get-tuple-element.13.partial, f32[16,128,128]{2,1,0:T(8,128)S(1)} %get-tuple-element.14.gates, ...), custom_call_target="tpu_custom_call" | custom-call | tf_op jit(solution)/shard_map/finish/pallas_call | solution.py:513

commit v4 on v3

--- a/solution.py
+++ b/solution.py
@@ -41,7 +41,7 @@
     streams, kept = refs[:6], refs[6:12]
     se, made, partial, gates, terms, starts, shift, carry, hops = refs[12:21]
     (
-        held, halo, arrived, sent, ext, extended, u_li, near, carried, own, inner, tally, lent, full,
+        held, halo, arrived, sent, ext, extended, u_li, near, hold, own, inner, tally, lent, full,
         se_feature, se_filter, li_feature, residue, rate, skip, in_sem, part_sem, fixed_sem, halo_send, halo_recv, pair_send, pair_recv, state_send, state_recv, swap_send, swap_recv, ready_sem,
     ) = refs[21:]
     rows, width = held.shape[1], held.shape[2]
@@ -57,7 +57,7 @@
     def device(index):
         return (dp, lax.div(index, chips), lax.rem(index, chips))
 
-    order = (4, 5, 1, 2, 0, 3)
+    order = (4, 5, 3, 1, 2, 0)
     parts = part_sem.shape[1]
     each = width // parts
     loads = [pltpu.make_async_copy(streams[i], held.at[i], in_sem.at[i]) for i in range(4)]
@@ -165,7 +165,7 @@
         if part == 0:
             for i in (3, 5, 0, 1):
                 fixed_loads[i].start()
-            for i in (1, 2, 0, 3):
+            for i in (3, 1, 2, 0):
                 loads[i].start()
             states(0, per // 2)
             meet()
@@ -202,6 +202,60 @@
         @pl.when(me > 0)
         def _():
             halo_copy(i).wait_recv()
+
+    def state_copy(source, target):
+        return pltpu.make_async_remote_copy(
+            src_ref=sent.at[pl.ds(lax.rem(target, pair) * half, half)],
+            dst_ref=arrived.at[source, pl.ds(lax.rem(target, pair) * half, half)],
+            send_sem=state_send.at[target],
+            recv_sem=state_recv.at[source],
+            device_id=device(target),
+            device_id_type=pl.DeviceIdType.MESH,
+        )
+
+    def pair_copy():
+        return pltpu.make_async_remote_copy(
+            src_ref=sent,
+            dst_ref=inner,
+            send_sem=pair_send.at[0],
+            recv_sem=pair_recv.at[0],
+            device_id=device(me + 1 - 2 * lax.rem(me, 2)),
+            device_id_type=pl.DeviceIdType.MESH,
+        )
+
+    for i in (3, 5, 0, 1):
+        fixed_loads[i].wait()
+
+    backward = -step
+
+    def filters(c, j):
+        cols = columns(c)
+        pace = rate[:, cols]
+        twice = 2.0 * pace
+        small = twice * (1.0 - twice * (0.5 - twice * (1.0 / 6.0 - twice * (1.0 / 24.0 - twice * (1.0 / 120.0)))))
+        gap = jnp.where(twice < 0.03125, small, 1.0 - jnp.exp(-twice))
+        rows_of = hold.at[j]
+        rows_of[pl.ds(0, modes)] = residue[:, cols] * jnp.sqrt(gap)
+        rows_of[pl.ds(modes, modes)] = jnp.exp(-pace)
+        hops[c] = jnp.exp(-pace * float(SUB))
+        total = jnp.zeros((SUB, LANES), jnp.float32)
+        for m in range(modes):
+            term = rows_of[pl.ds(m, 1)] * jnp.exp(rate[pl.ds(m, 1), cols] * backward)
+            total = total + term
+            terms[c, m] = term * rows_of[pl.ds(modes + m, 1)]
+        rows_of[pl.ds(2 * modes, SUB)] = total
+        for lag in range(SUB):
+            tap = rows_of[pl.ds(2 * modes + lag, 1)]
+            if lag == 0:
+                tap = tap + skip[:, cols]
+            near[c, lag] = jnp.where(place >= lag, jnp.broadcast_to(tap, (SUB, LANES)), 0.0)
+
+    twin = hold.shape[0]
+
+    @pl.loop(0, blocks // twin)
+    def _(many):
+        for j in range(twin):
+            filters(many * twin + j, j)
 
     ready(4)
     ready(5)
@@ -236,55 +290,23 @@
         for j in range(wide):
             fixed_up(many * wide + j, j)
 
-    def state_copy(source, target):
-        return pltpu.make_async_remote_copy(
-            src_ref=sent.at[pl.ds(lax.rem(target, pair) * half, half)],
-            dst_ref=arrived.at[source, pl.ds(lax.rem(target, pair) * half, half)],
-            send_sem=state_send.at[target],
-            recv_sem=state_recv.at[source],
-            device_id=device(target),
-            device_id_type=pl.DeviceIdType.MESH,
-        )
-
-    def pair_copy():
-        return pltpu.make_async_remote_copy(
-            src_ref=sent,
-            dst_ref=inner,
-            send_sem=pair_send.at[0],
-            recv_sem=pair_recv.at[0],
-            device_id=device(me + 1 - 2 * lax.rem(me, 2)),
-            device_id_type=pl.DeviceIdType.MESH,
-        )
-
     if pair == 2:
         @pl.when(lax.rem(me, 2) == 0)
         def _():
             pair_copy().start()
 
-    for i in (3, 5, 0, 1):
-        fixed_loads[i].wait()
+    loads[3].wait()
+    ready(3)
 
     @pl.loop(0, blocks)
     def _(c):
-        cols = columns(c)
-        pace = rate[:, cols]
-        twice = 2.0 * pace
-        small = twice * (1.0 - twice * (0.5 - twice * (1.0 / 6.0 - twice * (1.0 / 24.0 - twice * (1.0 / 120.0)))))
-        gap = jnp.where(twice < 0.03125, small, 1.0 - jnp.exp(-twice))
-        carried[c] = residue[:, cols] * jnp.sqrt(gap)
-        hops[c] = jnp.exp(-pace * float(SUB))
-        total = jnp.zeros((SUB, LANES), jnp.float32)
-        for m in range(modes):
-            speed = rate[pl.ds(m, 1), cols]
-            term = carried[c, pl.ds(m, 1)] * jnp.exp(-speed * step)
-            total = total + term
-            terms[c, m] = term * jnp.exp(-speed)
-        near[c, 0] = total
-        for lag in range(SUB - 1, -1, -1):
-            tap = near[c, 0, pl.ds(lag, 1)]
-            if lag == 0:
-                tap = tap + skip[:, cols]
-            near[c, lag] = jnp.where(place >= lag, jnp.broadcast_to(tap, (SUB, LANES)), 0.0)
+        gates[c] = featurized(3, c, li_feature, 0, 0)
+        taps = [near[c, lag] for lag in range(SUB)]
+        for a in range(chunks):
+            total = taps[0] * u_li[c, pl.ds(SUB + a * SUB, SUB)]
+            for lag in range(1, SUB):
+                total = total + taps[lag] * u_li[c, pl.ds(SUB + a * SUB - lag, SUB)]
+            partial[c, pl.ds(a * SUB, SUB)] = total
 
     if pair == 2:
         @pl.when(lax.rem(me, 2) == 1)
@@ -318,7 +340,7 @@
     else:
         send_states(me + 1, n)
 
-    for i in (1, 2, 0, 3):
+    for i in (1, 2, 0):
         loads[i].wait()
         ready(i)
 
@@ -331,13 +353,6 @@
         for lag in range(1, lags):
             mixed = mixed + se_filter[pl.ds(lag, 1), cols] * extended[pl.ds(SUB - lag, rows)]
         se[:, cols] = (featurized(0, c, se_feature, 0, 0) * mixed).astype(jnp.bfloat16)
-        gates[c] = featurized(3, c, li_feature, 0, 0)
-        taps = [near[c, lag] for lag in range(SUB)]
-        for a in range(chunks):
-            total = taps[0] * u_li[c, pl.ds(SUB + a * SUB, SUB)]
-            for lag in range(1, SUB):
-                total = total + taps[lag] * u_li[c, pl.ds(SUB + a * SUB - lag, SUB)]
-            partial[c, pl.ds(a * SUB, SUB)] = total
 
     odd = lax.rem(jnp.full((modes, LANES), me, jnp.int32), 2) == 1
     step_by = 4 if half % 4 == 0 else 1
@@ -487,7 +502,7 @@
             pltpu.VMEM((rows + SUB, LANES), f32),
             pltpu.VMEM((blocks, rows + SUB, LANES), f32),
             pltpu.VMEM((blocks, SUB, SUB, LANES), f32),
-            pltpu.VMEM((blocks, modes, LANES), f32),
+            pltpu.VMEM((2 if blocks % 2 == 0 else 1, 2 * modes + SUB, LANES), f32),
             pltpu.VMEM((blocks, modes, LANES), f32),
             pltpu.VMEM((blocks, modes, LANES), LINK),
             pltpu.VMEM((blocks, modes, LANES), f32),

time: 12.6 us -> 12.7 us (level)
  no operation moved by 1% of the time
where the time goes in v4:
time: 12.7 us; the launch traced here: 12.6 us
  Pallas kernels  11.9 us (94%)
  between operations  0.64 us (5%)
    pallas_call x1, Pallas kernels, shards(): pl.pallas_call(functools.partial(mixer, n, chips), out_shape=tuple((jax.S...  10.5 us
    pallas_call x1, Pallas kernels, shards(): pl.pallas_call(functools.partial(finish, n, chips), out_shape=(jax.ShapeD...  1.46 us

profile of v4, /device:TPU:5, one launch (start us, length us, event | category | flops | bytes accessed | tf_op | source)
XLA Modules:
  0.0 12.6 jit_solution(16601698369174510327)
XLA Ops:
  0.6 10.5 %mixer.1 = (bf16[128,2048]{1,0:T(8,128)(2,1)S(1)}, bf16[128,2048]{1,0:T(8,128)(2,1)S(1)}, f32[16,128,128]{2,1,0:T(8,128)S(1)}, f32[16,128,128]{2,1,0:T(8,128)S(1...) custom-call(bf16[128,2048]{1,0:T(8,128)(2,1)} %refs_0_.1, ...), custom_call_target="tpu_custom_call" | custom-call | tf_op jit(solution)/shard_map/mixer/pallas_call | solution.py:491
  11.1 1.5 %finish.1 = (bf16[128,2048]{1,0:T(8,128)(2,1)}, bf16[128,2048]{1,0:T(8,128)(2,1)}) custom-call(bf16[128,2048]{1,0:T(8,128)(2,1)S(1)} %get-tuple-element.11.se, bf16[128,2048]{1,0:T(8,128)(2,1)S(1)} %get-tuple-element.12.made, f32[16,128,128]{2,1,0:T(8,128)S(1)} %get-tuple-element.13.partial, f32[16,128,128]{2,1,0:T(8,128)S(1)} %get-tuple-element.14.gates, ...), custom_call_target="tpu_custom_call" | custom-call | tf_op jit(solution)/shard_map/finish/pallas_call | solution.py:528

commit v5 on v4

--- a/solution.py
+++ b/solution.py
@@ -157,6 +157,13 @@
         def _(c):
             local_states(c)
 
+    meet()
+
+    @pl.when(me < n - 1)
+    def _():
+        for i in order:
+            halo_copy(i).start()
+
     for i in (4, 2):
         fixed_loads[i].wait()
     for part in range(parts):
@@ -167,15 +174,7 @@
                 fixed_loads[i].start()
             for i in (3, 1, 2, 0):
                 loads[i].start()
-            states(0, per // 2)
-            meet()
-
-            @pl.when(me < n - 1)
-            def _():
-                for i in order:
-                    halo_copy(i).start()
-
-            states(per // 2, per)
+            states(0, per)
         else:
             states(part * per, (part + 1) * per)
 
@@ -222,6 +221,44 @@
             device_id=device(me + 1 - 2 * lax.rem(me, 2)),
             device_id_type=pl.DeviceIdType.MESH,
         )
+
+    ready(4)
+    ready(5)
+
+    wide = 4 if blocks % 4 == 0 else 1
+
+    def fixed_up(c, j):
+        cols = columns(c)
+
+        def opening(i, stream):
+            at = 2 * j + i - 4
+            ext[at, pl.ds(SUB, SUB)] = halo[i, :, cols].astype(jnp.float32)
+            ext[at, pl.ds(2 * SUB, SUB)] = held[i, pl.ds(0, SUB), cols].astype(jnp.float32)
+            total = li_feature[0, pl.ds(stream, 1), cols] * ext[at, pl.ds(2 * SUB, SUB)]
+            for lag in (1, 2):
+                total = total + li_feature[lag, pl.ds(stream, 1), cols] * ext[at, pl.ds(2 * SUB - lag, SUB)]
+            return total
+
+        right = (opening(4, 1) * opening(5, 2)).astype(jnp.bfloat16).astype(jnp.float32)
+        extended[pl.ds(j * SUB, SUB)] = right - u_li[c, pl.ds(SUB, SUB)]
+        u_li[c, pl.ds(SUB, SUB)] = right
+        pace = rate[:, cols]
+        moved = jnp.exp(-pace * float(SUB - 1)) * extended[pl.ds(j * SUB, 1)]
+        moved = moved + jnp.exp(-pace * float(SUB - 2)) * extended[pl.ds(j * SUB + 1, 1)]
+        shift[c] = moved
+        state = own[c] + jnp.exp(-pace * float(rows - SUB)) * moved
+        own[c] = state
+        sent[c] = state.astype(sent.dtype)
+
+    @pl.loop(0, blocks // wide)
+    def _(many):
+        for j in range(wide):
+            fixed_up(many * wide + j, j)
+
+    if pair == 2:
+        @pl.when(lax.rem(me, 2) == 0)
+        def _():
+            pair_copy().start()
 
     for i in (3, 5, 0, 1):
         fixed_loads[i].wait()
@@ -248,7 +285,7 @@
             tap = rows_of[pl.ds(2 * modes + lag, 1)]
             if lag == 0:
                 tap = tap + skip[:, cols]
-            near[c, lag] = jnp.where(place >= lag, jnp.broadcast_to(tap, (SUB, LANES)), 0.0)
+            near[c, pl.ds(lag, 1)] = tap
 
     twin = hold.shape[0]
 
@@ -257,66 +294,17 @@
         for j in range(twin):
             filters(many * twin + j, j)
 
-    ready(4)
-    ready(5)
-
-    wide = 4 if blocks % 4 == 0 else 1
-
-    def fixed_up(c, j):
-        cols = columns(c)
-
-        def opening(i, stream):
-            at = 2 * j + i - 4
-            ext[at, pl.ds(SUB, SUB)] = halo[i, :, cols].astype(jnp.float32)
-            ext[at, pl.ds(2 * SUB, SUB)] = held[i, pl.ds(0, SUB), cols].astype(jnp.float32)
-            total = li_feature[0, pl.ds(stream, 1), cols] * ext[at, pl.ds(2 * SUB, SUB)]
-            for lag in (1, 2):
-                total = total + li_feature[lag, pl.ds(stream, 1), cols] * ext[at, pl.ds(2 * SUB - lag, SUB)]
-            return total
-
-        right = (opening(4, 1) * opening(5, 2)).astype(jnp.bfloat16).astype(jnp.float32)
-        extended[pl.ds(j * SUB, SUB)] = right - u_li[c, pl.ds(SUB, SUB)]
-        u_li[c, pl.ds(SUB, SUB)] = right
-        pace = rate[:, cols]
-        moved = jnp.exp(-pace * float(SUB - 1)) * extended[pl.ds(j * SUB, 1)]
-        moved = moved + jnp.exp(-pace * float(SUB - 2)) * extended[pl.ds(j * SUB + 1, 1)]
-        shift[c] = moved
-        state = own[c] + jnp.exp(-pace * float(rows - SUB)) * moved
-        own[c] = state
-        sent[c] = state.astype(sent.dtype)
-
-    @pl.loop(0, blocks // wide)
-    def _(many):
-        for j in range(wide):
-            fixed_up(many * wide + j, j)
-
-    if pair == 2:
-        @pl.when(lax.rem(me, 2) == 0)
-        def _():
-            pair_copy().start()
-
-    loads[3].wait()
-    ready(3)
-
-    @pl.loop(0, blocks)
-    def _(c):
-        gates[c] = featurized(3, c, li_feature, 0, 0)
-        taps = [near[c, lag] for lag in range(SUB)]
-        for a in range(chunks):
-            total = taps[0] * u_li[c, pl.ds(SUB + a * SUB, SUB)]
-            for lag in range(1, SUB):
-                total = total + taps[lag] * u_li[c, pl.ds(SUB + a * SUB - lag, SUB)]
-            partial[c, pl.ds(a * SUB, SUB)] = total
-
     if pair == 2:
         @pl.when(lax.rem(me, 2) == 1)
         def _():
             pair_copy().wait_recv()
 
-            @pl.loop(0, blocks)
-            def _(c):
-                fall = jnp.exp(-rate[:, columns(c)] * float(rows))
-                sent[c] = (fall * inner[c].astype(jnp.float32) + own[c]).astype(sent.dtype)
+            @pl.loop(0, blocks // wide)
+            def _(many):
+                for j in range(wide):
+                    c = many * wide + j
+                    fall = jnp.exp(-rate[:, columns(c)] * float(rows))
+                    sent[c] = (fall * inner[c].astype(jnp.float32) + own[c]).astype(sent.dtype)
 
     leads = lax.rem(me, pair) == pair - 1
     slot = lax.div(me, pair)
@@ -339,6 +327,22 @@
         send_states(me + 3, n)
     else:
         send_states(me + 1, n)
+
+    loads[3].wait()
+    ready(3)
+
+    @pl.loop(0, blocks)
+    def _(c):
+        gates[c] = featurized(3, c, li_feature, 0, 0)
+        taps = [near[c, pl.ds(lag, 1)] for lag in range(SUB)]
+        for top in range(0, chunks, SUB):
+            count = min(SUB, chunks - top)
+            tokens = [u_li[c, pl.ds(SUB + top * SUB + b, count, SUB)] for b in range(SUB)]
+            for b in range(SUB):
+                total = taps[0] * tokens[b]
+                for lag in range(1, b + 1):
+                    total = total + taps[lag] * tokens[b - lag]
+                partial[c, pl.ds(top * SUB + b, count, SUB)] = total
 
     for i in (1, 2, 0):
         loads[i].wait()
@@ -501,7 +505,7 @@
             pltpu.VMEM((8, rows + 2 * SUB, LANES), f32),
             pltpu.VMEM((rows + SUB, LANES), f32),
             pltpu.VMEM((blocks, rows + SUB, LANES), f32),
-            pltpu.VMEM((blocks, SUB, SUB, LANES), f32),
+            pltpu.VMEM((blocks, SUB, LANES), f32),
             pltpu.VMEM((2 if blocks % 2 == 0 else 1, 2 * modes + SUB, LANES), f32),
             pltpu.VMEM((blocks, modes, LANES), f32),
             pltpu.VMEM((blocks, modes, LANES), LINK),

time: 12.7 us -> 12.4 us (0.976)
  Pallas kernels: 11.9 us -> 11.6 us
    pallas_call x1, Pallas kernels: 10.5 us -> 10.1 us  [shards(): pl.pallas_call(functools.partial(mixer, n, chips), out_shape=tuple((jax.S...]
where the time goes in v5:
time: 12.4 us; the launch traced here: 12.2 us
  Pallas kernels  11.6 us (94%)
  between operations  0.64 us (5%)
    pallas_call x1, Pallas kernels, shards(): pl.pallas_call(functools.partial(mixer, n, chips), out_shape=tuple((jax.S...  10.1 us
    pallas_call x1, Pallas kernels, shards(): pl.pallas_call(functools.partial(finish, n, chips), out_shape=(jax.ShapeD...  1.46 us

profile of v5, /device:TPU:5, one launch (start us, length us, event | category | flops | bytes accessed | tf_op | source)
XLA Modules:
  0.0 12.2 jit_solution(271864986016362293)
XLA Ops:
  0.6 10.1 %mixer.1 = (bf16[128,2048]{1,0:T(8,128)(2,1)S(1)}, bf16[128,2048]{1,0:T(8,128)(2,1)S(1)}, f32[16,128,128]{2,1,0:T(8,128)S(1)}, f32[16,128,128]{2,1,0:T(8,128)S(1...) custom-call(bf16[128,2048]{1,0:T(8,128)(2,1)} %refs_0_.1, ...), custom_call_target="tpu_custom_call" | custom-call | tf_op jit(solution)/shard_map/mixer/pallas_call | solution.py:495
  10.7 1.5 %finish.1 = (bf16[128,2048]{1,0:T(8,128)(2,1)}, bf16[128,2048]{1,0:T(8,128)(2,1)}) custom-call(bf16[128,2048]{1,0:T(8,128)(2,1)S(1)} %get-tuple-element.11.se, bf16[128,2048]{1,0:T(8,128)(2,1)S(1)} %get-tuple-element.12.made, f32[16,128,128]{2,1,0:T(8,128)S(1)} %get-tuple-element.13.partial, f32[16,128,128]{2,1,0:T(8,128)S(1)} %get-tuple-element.14.gates, ...), custom_call_target="tpu_custom_call" | custom-call | tf_op jit(solution)/shard_map/finish/pallas_call | solution.py:532

commit v6 on v5

--- a/solution.py
+++ b/solution.py
@@ -294,45 +294,10 @@
         for j in range(twin):
             filters(many * twin + j, j)
 
-    if pair == 2:
-        @pl.when(lax.rem(me, 2) == 1)
-        def _():
-            pair_copy().wait_recv()
-
-            @pl.loop(0, blocks // wide)
-            def _(many):
-                for j in range(wide):
-                    c = many * wide + j
-                    fall = jnp.exp(-rate[:, columns(c)] * float(rows))
-                    sent[c] = (fall * inner[c].astype(jnp.float32) + own[c]).astype(sent.dtype)
-
-    leads = lax.rem(me, pair) == pair - 1
-    slot = lax.div(me, pair)
-
-    def send_states(first, last):
-        @pl.when(leads)
-        def _():
-            @pl.loop(first, last)
-            def _(target):
-                state_copy(slot, target).start()
-
-    if pair == 2:
-        send_states(me + 1, jnp.minimum(me + 3, n))
-
-        if n > 4:
-            @pl.when(me == 1)
-            def _():
-                pl.semaphore_wait(ready_sem, 1)
-
-        send_states(me + 3, n)
-    else:
-        send_states(me + 1, n)
-
     loads[3].wait()
     ready(3)
 
-    @pl.loop(0, blocks)
-    def _(c):
+    def li_part(c):
         gates[c] = featurized(3, c, li_feature, 0, 0)
         taps = [near[c, pl.ds(lag, 1)] for lag in range(SUB)]
         for top in range(0, chunks, SUB):
@@ -343,6 +308,49 @@
                 for lag in range(1, b + 1):
                     total = total + taps[lag] * tokens[b - lag]
                 partial[c, pl.ds(top * SUB + b, count, SUB)] = total
+
+    middle = blocks // 2
+
+    @pl.loop(0, middle)
+    def _(c):
+        li_part(c)
+
+    if pair == 2:
+        @pl.when(lax.rem(me, 2) == 1)
+        def _():
+            pair_copy().wait_recv()
+
+            @pl.loop(0, blocks // wide)
+            def _(many):
+                for j in range(wide):
+                    c = many * wide + j
+                    fall = jnp.exp(-rate[:, columns(c)] * float(rows))
+                    sent[c] = (fall * inner[c].astype(jnp.float32) + own[c]).astype(sent.dtype)
+
+    leads = lax.rem(me, pair) == pair - 1
+    slot = lax.div(me, pair)
+
+    def send_states(first, last):
+        @pl.when(leads)
+        def _():
+            @pl.loop(first, last)
+            def _(target):
+                state_copy(slot, target).start()
+
+    if pair == 2:
+        send_states(me + 1, jnp.where(me == 1, min(4, n), n))
+    else:
+        send_states(me + 1, n)
+
+    @pl.loop(middle, blocks)
+    def _(c):
+        li_part(c)
+
+    if pair == 2 and n > 4:
+        @pl.when(me == 1)
+        def _():
+            pl.semaphore_wait(ready_sem, 1)
+            send_states(4, n)
 
     for i in (1, 2, 0):
         loads[i].wait()

time: 12.4 us -> 12.1 us (0.976)
  Pallas kernels: 11.6 us -> 11.3 us
    pallas_call x1, Pallas kernels: 10.1 us -> 9.82 us  [shards(): pl.pallas_call(functools.partial(mixer, n, chips), out_shape=tuple((jax.S...]
where the time goes in v6:
time: 12.1 us; the launch traced here: 11.9 us
  Pallas kernels  11.3 us (93%)
  between operations  0.64 us (5%)
    pallas_call x1, Pallas kernels, shards(): pl.pallas_call(functools.partial(mixer, n, chips), out_shape=tuple((jax.S...  9.82 us
    pallas_call x1, Pallas kernels, shards(): pl.pallas_call(functools.partial(finish, n, chips), out_shape=(jax.ShapeD...  1.46 us

profile of v6, /device:TPU:5, one launch (start us, length us, event | category | flops | bytes accessed | tf_op | source)
XLA Modules:
  0.0 11.9 jit_solution(795830420992678799)
XLA Ops:
  0.6 9.8 %mixer.1 = (bf16[128,2048]{1,0:T(8,128)(2,1)S(1)}, bf16[128,2048]{1,0:T(8,128)(2,1)S(1)}, f32[16,128,128]{2,1,0:T(8,128)S(1)}, f32[16,128,128]{2,1,0:T(8,128)S(1...) custom-call(bf16[128,2048]{1,0:T(8,128)(2,1)} %refs_0_.1, ...), custom_call_target="tpu_custom_call" | custom-call | tf_op jit(solution)/shard_map/mixer/pallas_call | solution.py:503
  10.5 1.5 %finish.1 = (bf16[128,2048]{1,0:T(8,128)(2,1)}, bf16[128,2048]{1,0:T(8,128)(2,1)}) custom-call(bf16[128,2048]{1,0:T(8,128)(2,1)S(1)} %get-tuple-element.11.se, bf16[128,2048]{1,0:T(8,128)(2,1)S(1)} %get-tuple-element.12.made, f32[16,128,128]{2,1,0:T(8,128)S(1)} %get-tuple-element.13.partial, f32[16,128,128]{2,1,0:T(8,128)S(1)} %get-tuple-element.14.gates, ...), custom_call_target="tpu_custom_call" | custom-call | tf_op jit(solution)/shard_map/finish/pallas_call | solution.py:540

commit v7 on v4

--- a/solution.py
+++ b/solution.py
@@ -167,15 +167,13 @@
                 fixed_loads[i].start()
             for i in (3, 1, 2, 0):
                 loads[i].start()
-            states(0, per // 2)
+            states(0, per)
             meet()
 
             @pl.when(me < n - 1)
             def _():
                 for i in order:
                     halo_copy(i).start()
-
-            states(per // 2, per)
         else:
             states(part * per, (part + 1) * per)
 
@@ -193,7 +191,6 @@
         @pl.when(lax.rem(me, 2) == 0)
         def _():
             inner[...] = jnp.zeros_like(inner)
-
 
     place = lax.broadcasted_iota(jnp.int32, (SUB, LANES), 0)
     step = place.astype(jnp.float32)
@@ -248,14 +245,18 @@
             tap = rows_of[pl.ds(2 * modes + lag, 1)]
             if lag == 0:
                 tap = tap + skip[:, cols]
-            near[c, lag] = jnp.where(place >= lag, jnp.broadcast_to(tap, (SUB, LANES)), 0.0)
+            near[c, pl.ds(lag, 1)] = tap
 
     twin = hold.shape[0]
 
-    @pl.loop(0, blocks // twin)
-    def _(many):
-        for j in range(twin):
-            filters(many * twin + j, j)
+    early = (lax.rem(me, chips) < pair) & (me >= pair)
+
+    @pl.when(early)
+    def _():
+        @pl.loop(0, blocks // twin)
+        def _(many):
+            for j in range(twin):
+                filters(many * twin + j, j)
 
     ready(4)
     ready(5)
@@ -295,28 +296,45 @@
         def _():
             pair_copy().start()
 
+    @pl.when(jnp.logical_not(early))
+    def _():
+        @pl.loop(0, blocks // twin)
+        def _(many):
+            for j in range(twin):
+                filters(many * twin + j, j)
+
     loads[3].wait()
     ready(3)
 
-    @pl.loop(0, blocks)
+    def li_part(c):
+        gates[c] = featurized(3, c, li_feature, 0, 0)
+        taps = [near[c, pl.ds(lag, 1)] for lag in range(SUB)]
+        for top in range(0, chunks, SUB):
+            count = min(SUB, chunks - top)
+            tokens = [u_li[c, pl.ds(SUB + top * SUB + b, count, SUB)] for b in range(SUB)]
+            for b in range(SUB):
+                total = taps[0] * tokens[b]
+                for lag in range(1, b + 1):
+                    total = total + taps[lag] * tokens[b - lag]
+                partial[c, pl.ds(top * SUB + b, count, SUB)] = total
+
+    middle = blocks // 2
+
+    @pl.loop(0, middle)
     def _(c):
-        gates[c] = featurized(3, c, li_feature, 0, 0)
-        taps = [near[c, lag] for lag in range(SUB)]
-        for a in range(chunks):
-            total = taps[0] * u_li[c, pl.ds(SUB + a * SUB, SUB)]
-            for lag in range(1, SUB):
-                total = total + taps[lag] * u_li[c, pl.ds(SUB + a * SUB - lag, SUB)]
-            partial[c, pl.ds(a * SUB, SUB)] = total
+        li_part(c)
 
     if pair == 2:
         @pl.when(lax.rem(me, 2) == 1)
         def _():
             pair_copy().wait_recv()
 
-            @pl.loop(0, blocks)
-            def _(c):
-                fall = jnp.exp(-rate[:, columns(c)] * float(rows))
-                sent[c] = (fall * inner[c].astype(jnp.float32) + own[c]).astype(sent.dtype)
+            @pl.loop(0, blocks // wide)
+            def _(many):
+                for j in range(wide):
+                    c = many * wide + j
+                    fall = jnp.exp(-rate[:, columns(c)] * float(rows))
+                    sent[c] = (fall * inner[c].astype(jnp.float32) + own[c]).astype(sent.dtype)
 
     leads = lax.rem(me, pair) == pair - 1
     slot = lax.div(me, pair)
@@ -329,16 +347,19 @@
                 state_copy(slot, target).start()
 
     if pair == 2:
-        send_states(me + 1, jnp.minimum(me + 3, n))
-
-        if n > 4:
-            @pl.when(me == 1)
-            def _():
-                pl.semaphore_wait(ready_sem, 1)
-
-        send_states(me + 3, n)
+        send_states(me + 1, jnp.where(me == 1, min(4, n), n))
     else:
         send_states(me + 1, n)
+
+    @pl.loop(middle, blocks)
+    def _(c):
+        li_part(c)
+
+    if pair == 2 and n > 4:
+        @pl.when(me == 1)
+        def _():
+            pl.semaphore_wait(ready_sem, 1)
+            send_states(4, n)
 
     for i in (1, 2, 0):
         loads[i].wait()
@@ -501,7 +522,7 @@
             pltpu.VMEM((8, rows + 2 * SUB, LANES), f32),
             pltpu.VMEM((rows + SUB, LANES), f32),
             pltpu.VMEM((blocks, rows + SUB, LANES), f32),
-            pltpu.VMEM((blocks, SUB, SUB, LANES), f32),
+            pltpu.VMEM((blocks, SUB, LANES), f32),
             pltpu.VMEM((2 if blocks % 2 == 0 else 1, 2 * modes + SUB, LANES), f32),
             pltpu.VMEM((blocks, modes, LANES), f32),
             pltpu.VMEM((blocks, modes, LANES), LINK),

time: 12.7 us -> 12 us (0.945)
  Pallas kernels: 11.9 us -> 11.2 us
    pallas_call x1, Pallas kernels: 10.5 us -> 9.75 us  [shards(): pl.pallas_call(functools.partial(mixer, n, chips), out_shape=tuple((jax.S...]
where the time goes in v7:
time: 12 us; the launch traced here: 11.8 us
  Pallas kernels  11.2 us (93%)
  between operations  0.64 us (5%)
    pallas_call x1, Pallas kernels, shards(): pl.pallas_call(functools.partial(mixer, n, chips), out_shape=tuple((jax.S...  9.75 us
    pallas_call x1, Pallas kernels, shards(): pl.pallas_call(functools.partial(finish, n, chips), out_shape=(jax.ShapeD...  1.46 us

profile of v7, /device:TPU:5, one launch (start us, length us, event | category | flops | bytes accessed | tf_op | source)
XLA Modules:
  0.0 11.8 jit_solution(12716673335226410254)
XLA Ops:
  0.6 9.7 %mixer.1 = (bf16[128,2048]{1,0:T(8,128)(2,1)S(1)}, bf16[128,2048]{1,0:T(8,128)(2,1)S(1)}, f32[16,128,128]{2,1,0:T(8,128)S(1)}, f32[16,128,128]{2,1,0:T(8,128)S(1...) custom-call(bf16[128,2048]{1,0:T(8,128)(2,1)} %refs_0_.1, ...), custom_call_target="tpu_custom_call" | custom-call | tf_op jit(solution)/shard_map/mixer/pallas_call | solution.py:512
  10.4 1.5 %finish.1 = (bf16[128,2048]{1,0:T(8,128)(2,1)}, bf16[128,2048]{1,0:T(8,128)(2,1)}) custom-call(bf16[128,2048]{1,0:T(8,128)(2,1)S(1)} %get-tuple-element.11.se, bf16[128,2048]{1,0:T(8,128)(2,1)S(1)} %get-tuple-element.12.made, f32[16,128,128]{2,1,0:T(8,128)S(1)} %get-tuple-element.13.partial, f32[16,128,128]{2,1,0:T(8,128)S(1)} %get-tuple-element.14.gates, ...), custom_call_target="tpu_custom_call" | custom-call | tf_op jit(solution)/shard_map/finish/pallas_call | solution.py:549

commit v8 on v7

--- a/solution.py
+++ b/solution.py
@@ -361,6 +361,20 @@
             pl.semaphore_wait(ready_sem, 1)
             send_states(4, n)
 
+    step_by = 4 if half % 4 == 0 else 1
+
+    def by_four(first, body):
+        @pl.loop(0, half // step_by)
+        def _(many):
+            for j in range(step_by):
+                body(first + many * step_by + j)
+
+    def cleared(c):
+        tally[c] = jnp.zeros((modes, LANES), jnp.float32)
+
+    ours, theirs = side * half, (pair - 1 - side) * half
+    by_four(ours, cleared)
+
     for i in (1, 2, 0):
         loads[i].wait()
         ready(i)
@@ -376,35 +390,20 @@
         se[:, cols] = (featurized(0, c, se_feature, 0, 0) * mixed).astype(jnp.bfloat16)
 
     odd = lax.rem(jnp.full((modes, LANES), me, jnp.int32), 2) == 1
-    step_by = 4 if half % 4 == 0 else 1
-
-    def by_four(first, body):
-        @pl.loop(0, half // step_by)
-        def _(many):
-            for j in range(step_by):
-                body(first + many * step_by + j)
-
-    def cleared(c):
-        tally[c] = jnp.zeros((modes, LANES), jnp.float32)
-
     def summed(source):
         def body(c):
             fall = jnp.exp(-rate[:, columns(c)] * float(rows * pair))
-            tally[c] = fall * tally[c] + arrived[source, c].astype(jnp.float32)
+            total = fall * tally[c] + arrived[source, c].astype(jnp.float32)
+            tally[c] = total
+            lent[c] = total.astype(lent.dtype)
 
         return body
-
-    def lend(c):
-        lent[c] = tally[c].astype(lent.dtype)
 
     def carried_in(c, before):
         if pair == 2:
             within = jnp.exp(-rate[:, columns(c)] * float(rows)) * before + inner[c].astype(jnp.float32)
             before = jnp.where(odd, within, before)
         carry[c] = before
-
-    ours, theirs = side * half, (pair - 1 - side) * half
-    by_four(ours, cleared)
 
     @pl.loop(0, slot)
     def _(source):
@@ -424,7 +423,6 @@
     if pair == 2:
         @pl.when(slot > 0)
         def _():
-            by_four(ours, lend)
             swap_copy(ours).start()
 
         @pl.when(slot == 0)

time: 12 us -> 12 us (level)
  no operation moved by 1% of the time
where the time goes in v8:
time: 12 us; the launch traced here: 11.8 us
  Pallas kernels  11.2 us (93%)
  between operations  0.64 us (5%)
    pallas_call x1, Pallas kernels, shards(): pl.pallas_call(functools.partial(mixer, n, chips), out_shape=tuple((jax.S...  9.74 us
    pallas_call x1, Pallas kernels, shards(): pl.pallas_call(functools.partial(finish, n, chips), out_shape=(jax.ShapeD...  1.46 us

profile of v8, /device:TPU:5, one launch (start us, length us, event | category | flops | bytes accessed | tf_op | source)
XLA Modules:
  0.0 11.8 jit_solution(18119569825968538869)
XLA Ops:
  0.6 9.7 %mixer.1 = (bf16[128,2048]{1,0:T(8,128)(2,1)S(1)}, bf16[128,2048]{1,0:T(8,128)(2,1)S(1)}, f32[16,128,128]{2,1,0:T(8,128)S(1)}, f32[16,128,128]{2,1,0:T(8,128)S(1...) custom-call(bf16[128,2048]{1,0:T(8,128)(2,1)} %refs_0_.1, ...), custom_call_target="tpu_custom_call" | custom-call | tf_op jit(solution)/shard_map/mixer/pallas_call | solution.py:510
  10.4 1.5 %finish.1 = (bf16[128,2048]{1,0:T(8,128)(2,1)}, bf16[128,2048]{1,0:T(8,128)(2,1)}) custom-call(bf16[128,2048]{1,0:T(8,128)(2,1)S(1)} %get-tuple-element.11.se, bf16[128,2048]{1,0:T(8,128)(2,1)S(1)} %get-tuple-element.12.made, f32[16,128,128]{2,1,0:T(8,128)S(1)} %get-tuple-element.13.partial, f32[16,128,128]{2,1,0:T(8,128)S(1)} %get-tuple-element.14.gates, ...), custom_call_target="tpu_custom_call" | custom-call | tf_op jit(solution)/shard_map/finish/pallas_call | solution.py:547

commit v9 on v8

--- a/solution.py
+++ b/solution.py
@@ -318,7 +318,7 @@
                     total = total + taps[lag] * tokens[b - lag]
                 partial[c, pl.ds(top * SUB + b, count, SUB)] = total
 
-    middle = blocks // 2
+    middle = 3 * blocks // 4
 
     @pl.loop(0, middle)
     def _(c):

time: 12 us -> 11.9 us (level)
  no operation moved by 1% of the time
where the time goes in v9:
time: 11.9 us; the launch traced here: 11.8 us
  Pallas kernels  11.1 us (93%)
  between operations  0.64 us (5%)
    pallas_call x1, Pallas kernels, shards(): pl.pallas_call(functools.partial(mixer, n, chips), out_shape=tuple((jax.S...  9.65 us
    pallas_call x1, Pallas kernels, shards(): pl.pallas_call(functools.partial(finish, n, chips), out_shape=(jax.ShapeD...  1.46 us

profile of v9, /device:TPU:5, one launch (start us, length us, event | category | flops | bytes accessed | tf_op | source)
XLA Modules:
  0.0 11.8 jit_solution(10556905234653554326)
XLA Ops:
  0.6 9.7 %mixer.1 = (bf16[128,2048]{1,0:T(8,128)(2,1)S(1)}, bf16[128,2048]{1,0:T(8,128)(2,1)S(1)}, f32[16,128,128]{2,1,0:T(8,128)S(1)}, f32[16,128,128]{2,1,0:T(8,128)S(1...) custom-call(bf16[128,2048]{1,0:T(8,128)(2,1)} %refs_0_.1, ...), custom_call_target="tpu_custom_call" | custom-call | tf_op jit(solution)/shard_map/mixer/pallas_call | solution.py:510
  10.3 1.5 %finish.1 = (bf16[128,2048]{1,0:T(8,128)(2,1)}, bf16[128,2048]{1,0:T(8,128)(2,1)}) custom-call(bf16[128,2048]{1,0:T(8,128)(2,1)S(1)} %get-tuple-element.11.se, bf16[128,2048]{1,0:T(8,128)(2,1)S(1)} %get-tuple-element.12.made, f32[16,128,128]{2,1,0:T(8,128)S(1)} %get-tuple-element.13.partial, f32[16,128,128]{2,1,0:T(8,128)S(1)} %get-tuple-element.14.gates, ...), custom_call_target="tpu_custom_call" | custom-call | tf_op jit(solution)/shard_map/finish/pallas_call | solution.py:547
